TPU v7x, 256 devices: a whole 4x4x8 slice. The times are simulated.
256 devices in a mesh: row: 4 (over x), col: 16 (over z, core), depth: 4 (over y).
Axes of the slice: x: 4, y: 4, z: 8, core: 2. Of those that a mesh axis runs over, the one named last changes fastest.
Arguments:
- amplitudes: float32 [8, 768, 6144], P('depth', 'col', 'row'), may hold values from -6 to 6
- integrals: float32 [8, 768, 16, 768], P('depth', 'row', 'col'), may hold values from -0.21875 to 0.21875
- irrep_virtual: int32 [768], replicated, may hold values from 0 to 7, as said below
- irrep_first: int32 [8], replicated, may hold values from 0 to 7
- irrep_second: int32 [8], replicated, may hold values from 0 to 7
- irrep_target: int32 [16], replicated, may hold values from 0 to 7
Outputs:
- cycle_term: float32 [16, 768, 6144], P('col', 'depth', 'row')
Inputs may be any that keep to these rules, and one draw needn't show every extreme that they name: `irrep_virtual`: labels never fall along the virtual orbitals, so each irrep is one contiguous block, the blocks in rising order of irrep; every irrep holds 64 or more virtuals.
All inputs are finite; a program needn't handle non-finite values.
Results may differ from a plain program's by a relative error of at most 0.0001.
Values sent between devices are 32-bit elements; how exact they have to be, the bound alone decides.
No kernel may reach another device: no remote copies, remote signals or barrier semaphores. Data moves between devices by JAX's collectives and lax.ppermute only.
A program may use at most 64 MiB of HBM per device.

v0:
```python
import jax
import jax.numpy as jnp
from jax import lax
from jax.sharding import PartitionSpec as P


def amp_mask(labels_k, labels_c, labels_x):
    parity = jnp.bitwise_xor(
        jnp.bitwise_xor(labels_k[:, None, None], labels_c[None, :, None]), labels_x[None, None, :]
    )
    return (parity == 0).astype(jnp.float32)


def int_mask(labels_k, labels_c, labels_j, labels_b):
    parity = jnp.bitwise_xor(
        jnp.bitwise_xor(labels_k[:, None, None, None], labels_c[None, :, None, None]),
        jnp.bitwise_xor(labels_j[None, None, :, None], labels_b[None, None, None, :]),
    )
    return (parity == 0).astype(jnp.float32)


def contract(left_amp, right_int):
    return jnp.einsum(
        "kcjb,kcx->jbx",
        right_int,
        left_amp,
        precision=lax.Precision.HIGHEST,
        preferred_element_type=jnp.float32,
    )


def per_device(amplitudes, integrals, irrep_virtual, irrep_first, irrep_second, irrep_target):
    k_local = amplitudes.shape[0]
    x_local = amplitudes.shape[2]
    j_local = integrals.shape[2]
    all_x = jnp.bitwise_xor(irrep_virtual[:, None], irrep_first[None, :]).reshape(-1)
    labels_k = lax.dynamic_slice_in_dim(irrep_second, lax.axis_index("depth") * k_local, k_local)
    labels_x = lax.dynamic_slice_in_dim(all_x, lax.axis_index("row") * x_local, x_local)
    labels_j = lax.dynamic_slice_in_dim(irrep_target, lax.axis_index("col") * j_local, j_local)
    gathered = lax.all_gather(amplitudes, "col", axis=1, tiled=True)
    gathered = gathered * amp_mask(labels_k, irrep_virtual, labels_x)
    masked = lax.all_gather(integrals, "row", axis=1, tiled=True) * int_mask(
        labels_k, irrep_virtual, labels_j, irrep_virtual
    )
    partial_sum = contract(gathered, masked)
    return lax.psum_scatter(partial_sum, "depth", scatter_dimension=1, tiled=True)


def solution(mesh):
    return jax.shard_map(
        per_device,
        mesh=mesh,
        in_specs=(P("depth", "col", "row"), P("depth", "row", "col", None), P(), P(), P(), P()),
        out_specs=P("col", "depth", "row"),
        check_vma=False,
    )
```

profile of v0, /device:TPU:1, one launch (start us, length us, event | category | flops | bytes accessed | tf_op | source)
XLA Modules:
  0.0 219.6 jit_solution(11587721565921521954)
XLA Ops:
  6.5 0.0 all-gather.3.cloned.1.call-start
  6.5 0.7 all-gather.3.cloned.1.call-update
  7.3 0.0 all-gather.5.cloned.1.call-start
  7.3 0.7 all-gather.5.cloned.1.call-update
  8.0 0.0 reduce-scatter.2.cloned.1.call-start
  8.1 0.9 broadcast_xor_fusion
  8.9 0.2 xor.105
  9.1 1.2 dynamic_slice.10
  10.4 0.7 dynamic_slice.9
  11.1 0.1 dynamic_slice.11
  11.2 1.3 broadcast_xor_fusion.2
  12.5 0.8 broadcast_xor_fusion.1
  13.3 54.6 %all-gather.3.cloned.1.call-done = f32[2,768,1,768]{3,2,1,0:T(1,128)} async-done(((f32[2,192,1,768]{3,2,1,0:T(1,128)}), f32[2,768,1,768]{3,2,1,0:T(1,128)}) %all-gather.3.cloned.1.call-update) | async-done | bytes 4718608 | tf_op jit(solution)/shard_map/all_gather | solution.py:42
  67.9 8.2 %compare_select_fusion = f32[2,768,1,768]{3,2,1,0:T(1,128)} fusion(f32[2,768,1,768]{3,2,1,0:T(1,128)} %all-gather.3.cloned.1.call-done, s32[768]{0:T(1024)S(1)} %broadcast_xor_fusion.2, s32[2,768]{1,0:T(2,128)S(1)} %broadcast_xor_fusion.1), kind=kLoop, calls=%fused_computation | loop fusion | flops 3538944 | bytes 9446400 | tf_op jit(solution)/shard_map/mul | solution.py:42
  76.1 55.5 %all-gather.5.cloned.1.call-done = f32[2,768,1536]{2,1,0:T(8,128)} async-done(((f32[2,48,1536]{2,1,0:T(8,128)}), f32[2,768,1536]{2,1,0:T(8,128)}) %all-gather.5.cloned.1.call-update) | async-done | bytes 9437200 | tf_op jit(solution)/shard_map/all_gather | solution.py:40
  131.6 29.5 %fusion.8 = f32[1,768,1536]{2,1,0:T(8,128)} fusion(f32[2,768,1536]{2,1,0:T(8,128)} %all-gather.5.cloned.1.call-done, s32[1536]{0:T(1024)S(1)} %dynamic_slice.11, s32[2,768]{1,0:T(2,128)S(1)} %broadcast_xor_fusion.1, f32[2,768,1,768]{3,2,1,0:T(1,128)} %compare_select_fusion), kind=kOutput, calls=%fused_computation.10 | convolution fusion | flops 21750349824 | bytes 18886656 | tf_op jit(solution)/shard_map/kcjb,kcx->jbx/dot_general | solution.py:23
  161.1 0.0 reduce-scatter.2.cloned.1.call-update
  161.1 51.9 %reduce-scatter.2.cloned.1.call-done = f32[1,192,1536]{2,1,0:T(8,128)} async-done(((f32[1,768,1536]{2,1,0:T(8,128)}), f32[1,192,1536]{2,1,0:T(8,128)}) %reduce-scatter.2.cloned.1.call-update) | async-done | bytes 1179664 | tf_op jit(solution)/shard_map/reduce_scatter | solution.py:46
Async XLA Ops:
  6.5 61.4 %all-gather.3.cloned.1.call-start = ((), (), s32[]{:S(2)}) async-start(), calls=%async_computation.1 | async-start | bytes 5898240 | tf_op jit(solution)/shard_map/all_gather | solution.py:42
  7.3 124.3 %all-gather.5.cloned.1.call-start = ((), (), s32[]{:S(2)}) async-start(), calls=%async_computation.2 | async-start | bytes 10027008 | tf_op jit(solution)/shard_map/all_gather | solution.py:40
  8.0 205.0 %reduce-scatter.2.cloned.1.call-start = ((), (), s32[]{:S(2)}) async-start(), calls=%async_computation.3 | async-start | bytes 5898240 | tf_op jit(solution)/shard_map/reduce_scatter | solution.py:46
Sparse Core Ops, SparseCore 0:
  9.1 58.7 all-gather.2
  69.7 61.7 all-gather.4
  161.2 51.7 reduce-scatter.1
where the time goes:
time: 220 us
  waiting for transfers between devices  164 us (75%)
  matrix products  29.5 us (13%)
  between operations  13.1 us (6%)
  other arithmetic  11.1 us (5%)
  local copies, waits for them, and re-layouts  2.25 us (1%)
    all_gather x1, waiting for transfers between devices, per_device(): gathered = lax.all_gather(amplitudes, 'col', axis=1, tiled=True)  55.5 us
    all_gather x1, waiting for transfers between devices, per_device(): lax.all_gather(integrals, 'row', axis=1, tiled=True)  54.6 us
    reduce_scatter x1, waiting for transfers between devices, per_device(): lax.psum_scatter(partial_sum, 'depth', scatter_dimension=1, tiled=True)  51.9 us
    dot_general x1, matrix products, contract(): jnp.einsum('kcjb,kcx->jbx', right_int, left_amp, precision=lax.Precision....  29.5 us
    mul x1, other arithmetic, per_device(): lax.all_gather(integrals, 'row', axis=1, tiled=True)  8.17 us
  transfers between devices with their start and end apart: 3, of which 3 were waited for; matrix products, arithmetic and copies ran while one was open for 6% of the time, Pallas kernels for 0%

commit v1 on v0

--- a/solution.py
+++ b/solution.py
@@ -37,7 +37,9 @@
     labels_k = lax.dynamic_slice_in_dim(irrep_second, lax.axis_index("depth") * k_local, k_local)
     labels_x = lax.dynamic_slice_in_dim(all_x, lax.axis_index("row") * x_local, x_local)
     labels_j = lax.dynamic_slice_in_dim(irrep_target, lax.axis_index("col") * j_local, j_local)
-    gathered = lax.all_gather(amplitudes, "col", axis=1, tiled=True)
+    gathered = jnp.concatenate(
+        lax.all_to_all(jnp.stack([amplitudes] * lax.axis_size("col")), "col", 0, 0), axis=1
+    )
     gathered = gathered * amp_mask(labels_k, irrep_virtual, labels_x)
     masked = lax.all_gather(integrals, "row", axis=1, tiled=True) * int_mask(
         labels_k, irrep_virtual, labels_j, irrep_virtual

time: 220 us -> 323 us (1.47)
  waiting for transfers between devices: 164 us -> 249 us
  starting transfers between devices: 0.08 us -> 10.2 us
  local copies, waits for them, and re-layouts: 2.25 us -> 11.7 us
  matrix products: 29.5 us -> 25.7 us
    all_to_all x0 -> x1, waiting for transfers between devices: none -> 139 us  [per_device(): lax.all_to_all(jnp.stack([amplitudes] * lax.axis_size('col')), 'col', 0, 0)]
    all_gather x1 -> x0, waiting for transfers between devices: 55.5 us -> none  [per_device(): gathered = lax.all_gather(amplitudes, 'col', axis=1, tiled=True)]
    all_to_all x0 -> x1, starting transfers between devices: none -> 10.1 us  [per_device(): lax.all_to_all(jnp.stack([amplitudes] * lax.axis_size('col')), 'col', 0, 0)]
    another operation x0 -> x1, local copies, waits for them, and re-layouts: none -> 5.9 us  [per_device(): jnp.stack([amplitudes] * lax.axis_size('col'))]
    all_to_all x0 -> x1, local copies, waits for them, and re-layouts: none -> 4.8 us  [per_device(): lax.all_to_all(jnp.stack([amplitudes] * lax.axis_size('col')), 'col', 0, 0)]
    mul x0 -> x1, other arithmetic: none -> 4.22 us  [per_device(): gathered = gathered * amp_mask(labels_k, irrep_virtual, labels_x)]
    dot_general x1, matrix products: 29.5 us -> 25.7 us  [contract(): jnp.einsum('kcjb,kcx->jbx', right_int, left_amp, precision=lax.Precision....]
  transfers between devices with their start and end apart: 3 -> 3, of which waited for: 3 -> 3; matrix products, arithmetic and copies ran while one was open for 6% -> 3% of each run, Pallas kernels for 0% -> 0%
where the time goes in v1:
time: 323 us
  waiting for transfers between devices  249 us (77%)
  matrix products  25.7 us (8%)
  between operations  13.5 us (4%)
  other arithmetic  13.3 us (4%)
  local copies, waits for them, and re-layouts  11.7 us (4%)
  starting transfers between devices  10.2 us (3%)
    all_to_all x1, waiting for transfers between devices, per_device(): lax.all_to_all(jnp.stack([amplitudes] * lax.axis_size('col')), 'col', 0, 0)  139 us
    all_gather x1, waiting for transfers between devices, per_device(): lax.all_gather(integrals, 'row', axis=1, tiled=True)  56 us
    reduce_scatter x1, waiting for transfers between devices, per_device(): lax.psum_scatter(partial_sum, 'depth', scatter_dimension=1, tiled=True)  53.3 us
    dot_general x1, matrix products, contract(): jnp.einsum('kcjb,kcx->jbx', right_int, left_amp, precision=lax.Precision....  25.7 us
    all_to_all x1, starting transfers between devices, per_device(): lax.all_to_all(jnp.stack([amplitudes] * lax.axis_size('col')), 'col', 0, 0)  10.1 us
    mul x1, other arithmetic, per_device(): lax.all_gather(integrals, 'row', axis=1, tiled=True)  8.16 us
  transfers between devices with their start and end apart: 3, of which 3 were waited for; matrix products, arithmetic and copies ran while one was open for 3% of the time, Pallas kernels for 0%

profile of v1, /device:TPU:1, one launch (start us, length us, event | category | flops | bytes accessed | tf_op | source)
XLA Modules:
  0.0 323.2 jit_solution(5010459104413232073)
XLA Ops:
  6.5 5.9 %stack.2 = f32[16,2,48,1536]{3,2,1,0:T(8,128)} broadcast(f32[2,48,1536]{2,1,0:T(8,128)} %param.6), dimensions={1,2,3} | broadcast | bytes 10027008 | tf_op jit(solution)/shard_map/stack | solution.py:41
  12.4 0.0 copy-start
  12.4 0.0 copy-start.1
  12.4 0.0 copy-start.2
  12.4 0.0 copy-start.3
  12.4 10.1 %all-to-all-start = ((f32[16,2,48,1536]{3,2,1,0:T(8,128)}), f32[16,2,48,1536]{3,2,1,0:T(8,128)}, u32[]{:S(2)}, u32[]{:S(2)}) async-start(f32[16,2,48,1536]{3,2,1,0:T(8,128)} %stack.2), calls=%async_computation | async-start | bytes 18874368 | tf_op jit(solution)/shard_map/all_to_all | solution.py:41
  22.6 0.0 all-gather.2.cloned.1.call-start
  22.6 0.7 all-gather.2.cloned.1.call-update
  23.3 0.0 reduce-scatter.2.cloned.1.call-start
  23.3 0.0 copy-done
  23.3 0.0 copy-done.1
  23.4 0.2 broadcast_xor_fusion
  23.5 0.2 xor.105
  23.7 0.1 dynamic_slice.11
  23.8 0.0 copy-done.2
  23.8 0.1 dynamic_slice.9
  23.9 0.0 copy-done.3
  23.9 0.6 dynamic_slice.10
  24.5 0.6 broadcast_xor_fusion.2
  25.1 0.1 broadcast_xor_fusion.1
  25.2 56.0 %all-gather.2.cloned.1.call-done = f32[2,768,1,768]{3,2,1,0:T(1,128)} async-done(((f32[2,192,1,768]{3,2,1,0:T(1,128)}), f32[2,768,1,768]{3,2,1,0:T(1,128)}) %all-gather.2.cloned.1.call-update) | async-done | bytes 4718608 | tf_op jit(solution)/shard_map/all_gather | solution.py:44
  81.2 8.2 %compare_select_fusion = f32[2,768,1,768]{3,2,1,0:T(1,128)} fusion(f32[2,768,1,768]{3,2,1,0:T(1,128)} %all-gather.2.cloned.1.call-done, s32[768]{0:T(1024)S(1)} %broadcast_xor_fusion.2, s32[2,768]{1,0:T(2,128)S(1)} %broadcast_xor_fusion.1), kind=kLoop, calls=%fused_computation | loop fusion | flops 3538944 | bytes 9446400 | tf_op jit(solution)/shard_map/mul | solution.py:44
  89.3 139.1 %all-to-all-done = f32[16,2,48,1536]{3,2,1,0:T(8,128)} async-done(((f32[16,2,48,1536]{3,2,1,0:T(8,128)}), f32[16,2,48,1536]{3,2,1,0:T(8,128)}, u32[]{:S(2)}, u32[]{:S(2)}) %all-to-all-start) | async-done | bytes 9437216 | tf_op jit(solution)/shard_map/all_to_all | solution.py:41
  228.4 0.0 slice-start
  228.4 4.8 %copy.10 = f32[16,2,48,1536]{3,2,0,1:T(8,128)S(1)} copy(f32[16,2,48,1536]{3,2,1,0:T(8,128)} %all-to-all-done) | data formatting | bytes 18874368 | tf_op jit(solution)/shard_map/all_to_all | solution.py:41
  233.2 0.0 slice-start.1
  233.2 4.2 %bitcast_select_fusion = f32[2,768,1536]{2,1,0:T(8,128)} fusion(f32[16,2,48,1536]{3,2,0,1:T(8,128)S(1)} %copy.10, s32[1536]{0:T(1024)S(1)} %dynamic_slice.11, s32[2,768]{1,0:T(2,128)S(1)} %broadcast_xor_fusion.1), kind=kLoop, calls=%fused_computation.1 | loop fusion | flops 7077888 | bytes 18886656 | tf_op jit(solution)/shard_map/mul | solution.py:43
  237.4 0.0 slice-done
  237.4 0.0 slice-done.1
  237.4 25.7 %fusion.3 = f32[1,768,1536]{2,1,0:T(8,128)} fusion(f32[2,768,1536]{2,1,0:T(8,128)} %bitcast_select_fusion, f32[2,768,1,768]{3,2,1,0:T(1,128)S(1)} %bitcast.16), kind=kOutput, calls=%fused_computation.6 | convolution fusion | flops 21743271936 | bytes 18874368 | tf_op jit(solution)/shard_map/kcjb,kcx->jbx/dot_general | solution.py:23
  263.1 0.0 reduce-scatter.2.cloned.1.call-update
  263.1 53.3 %reduce-scatter.2.cloned.1.call-done = f32[1,192,1536]{2,1,0:T(8,128)} async-done(((f32[1,768,1536]{2,1,0:T(8,128)}), f32[1,192,1536]{2,1,0:T(8,128)}) %reduce-scatter.2.cloned.1.call-update) | async-done | bytes 1179664 | tf_op jit(solution)/shard_map/reduce_scatter | solution.py:48
  (1 shorter events, 0.0 us)
Async XLA Ops:
  12.4 10.9 %copy-start = (s32[768]{0:T(1024)S(1)}, s32[768]{0:T(1024)}, u32[]{:S(2)}) copy-start(s32[768]{0:T(1024)} %param.8) | copy-start | bytes 9220
  12.4 10.9 %copy-start.1 = (s32[8]{0:T(128)S(1)}, s32[8]{0:T(128)}, u32[]{:S(2)}) copy-start(s32[8]{0:T(128)} %param.9) | copy-start | bytes 100
  12.4 11.4 %copy-start.2 = (s32[8]{0:T(128)S(1)}, s32[8]{0:T(128)}, u32[]{:S(2)}) copy-start(s32[8]{0:T(128)} %param.10) | copy-start | bytes 100
  12.4 11.5 %copy-start.3 = (s32[16]{0:T(128)S(1)}, s32[16]{0:T(128)}, u32[]{:S(2)}) copy-start(s32[16]{0:T(128)} %param.11) | copy-start | bytes 196
  12.4 215.9 %all-to-all-start = ((f32[16,2,48,1536]{3,2,1,0:T(8,128)}), f32[16,2,48,1536]{3,2,1,0:T(8,128)}, u32[]{:S(2)}, u32[]{:S(2)}) async-start(f32[16,2,48,1536]{3,2,1,0:T(8,128)} %stack.2), calls=%async_computation | async-start | bytes 18874368 | tf_op jit(solution)/shard_map/all_to_all | solution.py:41
  22.6 58.6 %all-gather.2.cloned.1.call-start = ((), (), s32[]{:S(2)}) async-start(), calls=%async_computation.2 | async-start | bytes 5898240 | tf_op jit(solution)/shard_map/all_gather | solution.py:44
  23.3 293.1 %reduce-scatter.2.cloned.1.call-start = ((), (), s32[]{:S(2)}) async-start(), calls=%async_computation.3 | async-start | bytes 5898240 | tf_op jit(solution)/shard_map/reduce_scatter | solution.py:48
  228.4 9.0 %slice-start = ((s8[4718592]{0:T(1024)(128)(4,1)}), s8[4194304]{0:T(1024)(128)(4,1)S(1)}, s32[]{:S(2)}) async-start(s8[4718592]{0:T(1024)(128)(4,1)} %bitcast.15), calls=%async_computation.4 | async-start | bytes 8388608
  233.2 4.2 %slice-start.1 = ((s8[4718592]{0:T(1024)(128)(4,1)}), s8[524288]{0:T(1024)(128)(4,1)S(1)}, s32[]{:S(2)}) async-start(s8[4718592]{0:T(1024)(128)(4,1)} %bitcast.15), calls=%async_computation.5 | async-start | bytes 1048576
Sparse Core Ops, SparseCore 0:
  25.2 55.9 all-gather.1
  263.2 53.0 reduce-scatter.1
